TPU v7x, 32 devices: a whole 2x2x4 slice. The times are simulated.
32 devices in a mesh: grp: 2 (over core), edge: 4 (over z), gate: 4 (over y, x).
Axes of the slice: x: 2, y: 2, z: 4, core: 2. Of those that a mesh axis runs over, the one named last changes fastest.
Arguments:
- node_feat: bfloat16 [19456, 16], P(('grp', 'edge')), may hold values from -6 to 6
- dist_feat: bfloat16 [39936, 12], P(('grp', 'edge')), may hold values from -6 to 6
- bond: int32 [39936], P(('grp', 'edge')), may hold values from 0 to 3
- source: int32 [39936], P(('grp', 'edge')), may hold values from 0 to 2431, as said below
- target_node: int32 [39936], P(('grp', 'edge')), may hold values from 0 to 2431, as said below
- mol_id: int32 [19456], P(('grp', 'edge')), may hold values from 0 to 127, as said below
- flag: int32 [1024], P(('grp', 'edge')), may hold values 0 or 1
- target: float32 [1024, 12], P(('grp', 'edge')), may hold values from -6 to 6
- embed_weight: float32 [16, 128], P(None, 'gate'), may hold values from -1.5 to 1.5
- edge_first: float32 [17, 128], replicated, may hold values from -1.5 to 1.5
- edge_second: float32 [129, 16384], P(None, 'gate'), may hold values from -0.046875 to 0.046875
- gru_weight: float32 [2, 129, 3, 128], P(None, None, None, 'gate'), may hold values from -0.5 to 0.5
- set_lstm: float32 [385, 512], replicated, may hold values from -0.3125 to 0.3125
- head_weight: float32 [257, 12], replicated, may hold values from -0.375 to 0.375
- mom_embed: float32 [16, 128], P(None, 'gate'), may hold values from -3.8146973e-06 to 3.8146973e-06
- mom_first: float32 [17, 128], replicated, may hold values from -3.8146973e-06 to 3.8146973e-06
- mom_second: float32 [129, 16384], P(None, 'gate'), may hold values from -3.8146973e-06 to 3.8146973e-06
- mom_gru: float32 [2, 129, 3, 128], P(None, None, None, 'gate'), may hold values from -3.8146973e-06 to 3.8146973e-06
- mom_lstm: float32 [385, 512], replicated, may hold values from -3.8146973e-06 to 3.8146973e-06
- mom_head: float32 [257, 12], replicated, may hold values from -3.8146973e-06 to 3.8146973e-06
- var_embed: float32 [16, 128], P(None, 'gate'), may hold values from 4.137299e-14 to 1.6549196e-13
- var_first: float32 [17, 128], replicated, may hold values from 4.137299e-14 to 1.6549196e-13
- var_second: float32 [129, 16384], P(None, 'gate'), may hold values from 4.137299e-14 to 1.6549196e-13
- var_gru: float32 [2, 129, 3, 128], P(None, None, None, 'gate'), may hold values from 4.137299e-14 to 1.6549196e-13
- var_lstm: float32 [385, 512], replicated, may hold values from 4.137299e-14 to 1.6549196e-13
- var_head: float32 [257, 12], replicated, may hold values from 4.137299e-14 to 1.6549196e-13
- step_count: int32 [1], replicated, may hold values from 2 to 20
Outputs:
- loss: float32 [], replicated
- grad_norm: float32 [], replicated
- embed_out: float32 [16, 128], P(None, 'gate')
- first_out: float32 [17, 128], replicated
- second_out: float32 [129, 16384], P(None, 'gate')
- gru_out: float32 [2, 129, 3, 128], P(None, None, None, 'gate')
- lstm_out: float32 [385, 512], replicated
- head_out: float32 [257, 12], replicated
- embed_mom: float32 [16, 128], P(None, 'gate')
- first_mom: float32 [17, 128], replicated
- second_mom: float32 [129, 16384], P(None, 'gate')
- gru_mom: float32 [2, 129, 3, 128], P(None, None, None, 'gate')
- lstm_mom: float32 [385, 512], replicated
- head_mom: float32 [257, 12], replicated
- embed_var: float32 [16, 128], P(None, 'gate')
- first_var: float32 [17, 128], replicated
- second_var: float32 [129, 16384], P(None, 'gate')
- gru_var: float32 [2, 129, 3, 128], P(None, None, None, 'gate')
- lstm_var: float32 [385, 512], replicated
- head_var: float32 [257, 12], replicated
Inputs may be any that keep to these rules, and one draw needn't show every extreme that they name: `mol_id`: within each group of 2432 atoms the molecule ids never fall and every molecule of 0 to 127 has at least one atom. `source`: an atom of the edge's own group. `target_node`: an atom of the same group and molecule as the edge's source.
All inputs are finite; a program needn't handle non-finite values. No bound on the sum of `flag` on one device may be relied on, other than what follows from the above.
Results may differ from a plain program's by a relative error of at most 0.005.
The roundings to bfloat16 on the way count: a program that leaves them out, or rounds other values in their place, can miss the bound.
Values may be sent and summed in bfloat16 or wider, within the bound.
No kernel may reach another device: no remote copies, remote signals or barrier semaphores. Data moves between devices by JAX's collectives and lax.ppermute only.
A program may use at most 256 MiB of HBM per device.

v0:
```python
import jax
import jax.numpy as jnp
from jax import lax
from jax.sharding import PartitionSpec as P

H = 128
EDGE_HID = 128
NT = 12
BONDS = 4
STEPS = 3
SET_STEPS = 6
MOL_DEV = 128
EIN = 16
EDGE_BLOCK = 384


HIGH = lax.Precision.HIGHEST
CLIP = 0.01
BETA_ONE = 0.9
BETA_TWO = 0.999
EPSILON = 1e-08
DECAY = 0.01
RATES = (0.1, 0.05, 0.005, 0.02, 0.02, 0.02)


def fdot(left, right):
    return jnp.dot(left, right, precision=HIGH, preferred_element_type=jnp.float32)


def bdot(left, right):
    return jnp.dot(left, right, preferred_element_type=jnp.float32)


def tdot(left, right, exact=False):
    return lax.dot_general(
        left,
        right,
        (((0,), (0,)), ((), ())),
        precision=HIGH if exact else None,
        preferred_element_type=jnp.float32,
    )


def ndot(left, right):
    return lax.dot_general(
        left, right, (((1,), (1,)), ((), ())), preferred_element_type=jnp.float32
    )


def gru_cell(gate_in, gate_hid, state):
    reset = jax.nn.sigmoid(gate_in[:, 0] + gate_hid[:, 0])
    update = jax.nn.sigmoid(gate_in[:, 1] + gate_hid[:, 1])
    fresh = jnp.tanh(gate_in[:, 2] + reset * gate_hid[:, 2])
    return (1.0 - update) * fresh + update * state


def mask_weights(flag):
    columns = jnp.arange(NT)[None, :]
    return jnp.maximum(flag[:, None], (columns < NT // 2).astype(jnp.int32)).astype(jnp.float32)


def readout(hidden, mol_id, set_lstm, head_weight):
    member = (mol_id[:, None] == jnp.arange(MOL_DEV)[None, :]).astype(jnp.float32)
    query = jnp.zeros((MOL_DEV, H), jnp.float32)
    cell = jnp.zeros((MOL_DEV, H), jnp.float32)
    qstar = jnp.zeros((MOL_DEV, 2 * H), jnp.float32)
    for rounds in range(SET_STEPS):
        gates = (
            fdot(qstar, set_lstm[: 2 * H]) + fdot(query, set_lstm[2 * H : 3 * H]) + set_lstm[3 * H]
        )
        cell = jax.nn.sigmoid(gates[:, H : 2 * H]) * cell + jax.nn.sigmoid(gates[:, :H]) * jnp.tanh(
            gates[:, 2 * H : 3 * H]
        )
        query = jax.nn.sigmoid(gates[:, 3 * H :]) * jnp.tanh(cell)
        scores = jnp.sum(hidden * fdot(member, query), axis=1)
        peak = jnp.max(jnp.where(member > 0, scores[:, None], -jnp.inf), axis=0)
        expo = jnp.exp(scores - fdot(member, peak))
        totals = fdot(expo, member)
        weight = expo / fdot(member, totals)
        summary = jnp.einsum("nm,nh->mh", member, weight[:, None] * hidden, precision=HIGH)
        qstar = jnp.concatenate([query, summary], axis=1)
    return fdot(qstar, head_weight[: 2 * H]) + head_weight[2 * H]


def adamw(weight, grad, mom, var, rate, count):
    mom_new = BETA_ONE * mom + (1.0 - BETA_ONE) * grad
    var_new = BETA_TWO * var + (1.0 - BETA_TWO) * grad * grad
    mom_hat = mom_new / (1.0 - BETA_ONE**count)
    var_hat = var_new / (1.0 - BETA_TWO**count)
    return (
        weight - rate * (mom_hat / (jnp.sqrt(var_hat) + EPSILON) + DECAY * weight),
        mom_new,
        var_new,
    )


def bond_onehot(bond_rows):
    return (bond_rows[:, None] == jnp.arange(BONDS)[None, :]).astype(jnp.float32)


def gather_hidden(state):
    return lax.all_gather(state.astype(jnp.bfloat16), "gate", axis=1, tiled=True)


def on_device(
    node_feat,
    dist_feat,
    bond,
    source,
    target_node,
    mol_id,
    flag,
    target,
    embed_weight,
    edge_first,
    edge_second,
    gru_weight,
    set_lstm,
    head_weight,
    mom_embed,
    mom_first,
    mom_second,
    mom_gru,
    mom_lstm,
    mom_head,
    var_embed,
    var_first,
    var_second,
    var_gru,
    var_lstm,
    var_head,
    step_count,
):
    nodes = node_feat.shape[0]
    width = embed_weight.shape[1]
    blocks = source.shape[0] // EDGE_BLOCK

    def split_rows(array):
        return array.reshape((blocks, EDGE_BLOCK) + array.shape[1:])

    edge_pre = (
        fdot(bond_onehot(bond), edge_first[:BONDS])
        + fdot(dist_feat.astype(jnp.float32), edge_first[BONDS:EIN])
        + edge_first[EIN]
    )
    edge_low = jax.nn.silu(edge_pre).astype(jnp.bfloat16)
    second_low = edge_second[:EDGE_HID].astype(jnp.bfloat16)
    second_bias = edge_second[EDGE_HID]
    gru_low = gru_weight[:, :H].reshape(2, H, 3 * width).astype(jnp.bfloat16)
    all_mats = (
        (bdot(edge_low, second_low) + second_bias)
        .astype(jnp.bfloat16)
        .reshape(source.shape[0], width, H)
    )
    block_data = (split_rows(all_mats), split_rows(source), split_rows(target_node))
    state = bdot(node_feat, embed_weight.astype(jnp.bfloat16))
    kept = []
    for step in range(STEPS):
        hidden_full = gather_hidden(state)

        def send_one_block(total, pieces):
            mats, src_rows, tgt_rows = pieces
            parts = jnp.einsum(
                "eoi,ei->eo", mats, hidden_full[src_rows], preferred_element_type=jnp.float32
            )
            return (total + jax.ops.segment_sum(parts, tgt_rows, num_segments=nodes), None)

        msg_slice = lax.scan(send_one_block, jnp.zeros((nodes, width), jnp.float32), block_data)[0]
        message_full = lax.all_gather(msg_slice.astype(jnp.bfloat16), "gate", axis=1, tiled=True)
        gate_in = bdot(message_full, gru_low[0]).reshape(nodes, 3, width) + gru_weight[0, H]
        gate_hid = bdot(hidden_full, gru_low[1]).reshape(nodes, 3, width) + gru_weight[1, H]
        kept.append((hidden_full, message_full, gate_in, gate_hid, state))
        state = gru_cell(gate_in, gate_hid, state)
    hidden_last = gather_hidden(state)
    present = mask_weights(flag)
    count = lax.psum(jnp.sum(present), ("grp", "edge"))

    def local_loss(hidden_vals, lstm, headw):
        pred = readout(hidden_vals, mol_id, lstm, headw)
        return jnp.sum(present * (pred - target) ** 2) / count

    loss_part, pullback = jax.vjp(
        local_loss, hidden_last.astype(jnp.float32), set_lstm, head_weight
    )
    d_hidden, grad_lstm, grad_head = pullback(jnp.ones((), jnp.float32))
    d_state = lax.dynamic_slice_in_dim(d_hidden, lax.axis_index("gate") * width, width, 1)
    grad_in = jnp.zeros((H, 3 * width), jnp.float32)
    grad_hid = jnp.zeros((H, 3 * width), jnp.float32)
    bias_in = jnp.zeros((3 * width,), jnp.float32)
    bias_hid = jnp.zeros((3 * width,), jnp.float32)
    returned = []
    for step in reversed(range(STEPS)):
        hidden_full, message_full, gate_in, gate_hid, previous = kept[step]
        cell_back = jax.vjp(gru_cell, gate_in, gate_hid, previous)[1]
        d_gin, d_ghid, d_direct = cell_back(d_state)
        d_gin_low = d_gin.reshape(nodes, 3 * width).astype(jnp.bfloat16)
        d_ghid_low = d_ghid.reshape(nodes, 3 * width).astype(jnp.bfloat16)
        grad_in = grad_in + tdot(message_full, d_gin_low)
        grad_hid = grad_hid + tdot(hidden_full, d_ghid_low)
        bias_in = bias_in + jnp.sum(d_gin_low.astype(jnp.float32), axis=0)
        bias_hid = bias_hid + jnp.sum(d_ghid_low.astype(jnp.float32), axis=0)
        d_message = lax.psum_scatter(
            ndot(d_gin_low, gru_low[0]), "gate", scatter_dimension=1, tiled=True
        )
        d_msg_low = d_message.astype(jnp.bfloat16)

        def return_one_block(total, pieces):
            mats, src_rows, tgt_rows = pieces
            parts = jnp.einsum(
                "eoi,eo->ei", mats, d_msg_low[tgt_rows], preferred_element_type=jnp.float32
            )
            return (total + jax.ops.segment_sum(parts, src_rows, num_segments=nodes), None)

        d_hidden_part = (
            ndot(d_ghid_low, gru_low[1])
            + lax.scan(return_one_block, jnp.zeros((nodes, H), jnp.float32), block_data)[0]
        )
        d_state = d_direct + lax.psum_scatter(
            d_hidden_part, "gate", scatter_dimension=1, tiled=True
        )
        returned.insert(0, d_msg_low)
    grad_embed = tdot(node_feat, d_state.astype(jnp.bfloat16))
    msg_stack = jnp.stack(returned)
    hid_stack = jnp.stack([item[0] for item in kept])

    def final_block(carry, pieces):
        grad_wide, grad_bias, grad_first = carry
        edge_rows, src_rows, tgt_rows, pre_rows, bond_rows, dist_rows = pieces
        mats_grad = jnp.einsum(
            "teo,tei->eoi",
            msg_stack[:, tgt_rows],
            hid_stack[:, src_rows],
            preferred_element_type=jnp.float32,
        )
        flat_low = mats_grad.reshape(edge_rows.shape[0], width * H).astype(jnp.bfloat16)
        grad_wide = grad_wide + tdot(edge_rows, flat_low)
        grad_bias = grad_bias + jnp.sum(flat_low.astype(jnp.float32), axis=0)
        sigma = jax.nn.sigmoid(pre_rows)
        d_pre = ndot(flat_low, second_low) * sigma * (1.0 + pre_rows * (1.0 - sigma))
        rows_grad = jnp.concatenate(
            [
                tdot(bond_onehot(bond_rows), d_pre, True),
                tdot(dist_rows.astype(jnp.float32), d_pre, True),
                jnp.sum(d_pre, axis=0)[None],
            ],
            axis=0,
        )
        return ((grad_wide, grad_bias, grad_first + rows_grad), None)

    start = (
        jnp.zeros((EDGE_HID, width * H), jnp.float32),
        jnp.zeros((width * H,), jnp.float32),
        jnp.zeros((EIN + 1, EDGE_HID), jnp.float32),
    )
    final_data = (
        split_rows(edge_low),
        split_rows(source),
        split_rows(target_node),
        split_rows(edge_pre),
        split_rows(bond),
        split_rows(dist_feat),
    )
    grad_wide, grad_bias, grad_first = lax.scan(final_block, start, final_data)[0]
    grad_first = lax.psum(grad_first, "gate")
    grad_second = jnp.concatenate([grad_wide, grad_bias[None]], axis=0)
    grad_gru = jnp.stack(
        [
            jnp.concatenate([grad_in, bias_in[None]], axis=0),
            jnp.concatenate([grad_hid, bias_hid[None]], axis=0),
        ]
    ).reshape(2, H + 1, 3, width)
    local_grads = (grad_embed, grad_first, grad_second, grad_gru, grad_lstm, grad_head, loss_part)
    summed = lax.psum(
        (
            local_grads[0],
            local_grads[1],
            local_grads[2],
            local_grads[3],
            local_grads[4],
            local_grads[5],
            local_grads[6],
        ),
        ("grp", "edge"),
    )
    grads = summed[:6]
    loss = summed[6]
    split_sq = (
        jnp.sum(grads[0] * grads[0]) + jnp.sum(grads[2] * grads[2]) + jnp.sum(grads[3] * grads[3])
    )
    whole_sq = (
        jnp.sum(grads[1] * grads[1]) + jnp.sum(grads[4] * grads[4]) + jnp.sum(grads[5] * grads[5])
    )
    norm = jnp.sqrt(lax.psum(split_sq, "gate") + whole_sq)
    factor = jnp.minimum(1.0, CLIP / norm)
    params = (embed_weight, edge_first, edge_second, gru_weight, set_lstm, head_weight)
    moms = (mom_embed, mom_first, mom_second, mom_gru, mom_lstm, mom_head)
    varis = (var_embed, var_first, var_second, var_gru, var_lstm, var_head)
    stepno = step_count[0].astype(jnp.float32)
    results = [
        adamw(params[index], grads[index] * factor, moms[index], varis[index], RATES[index], stepno)
        for index in range(6)
    ]
    return (
        loss,
        norm,
        results[0][0],
        results[1][0],
        results[2][0],
        results[3][0],
        results[4][0],
        results[5][0],
        results[0][1],
        results[1][1],
        results[2][1],
        results[3][1],
        results[4][1],
        results[5][1],
        results[0][2],
        results[1][2],
        results[2][2],
        results[3][2],
        results[4][2],
        results[5][2],
    )


def solution(mesh):
    return jax.shard_map(
        on_device,
        mesh=mesh,
        in_specs=(
            P(("grp", "edge"), None),
            P(("grp", "edge"), None),
            P(("grp", "edge")),
            P(("grp", "edge")),
            P(("grp", "edge")),
            P(("grp", "edge")),
            P(("grp", "edge")),
            P(("grp", "edge"), None),
            P(None, "gate"),
            P(),
            P(None, "gate"),
            P(None, None, None, "gate"),
            P(),
            P(),
            P(None, "gate"),
            P(),
            P(None, "gate"),
            P(None, None, None, "gate"),
            P(),
            P(),
            P(None, "gate"),
            P(),
            P(None, "gate"),
            P(None, None, None, "gate"),
            P(),
            P(),
            P(),
        ),
        out_specs=(
            P(),
            P(),
            P(None, "gate"),
            P(),
            P(None, "gate"),
            P(None, None, None, "gate"),
            P(),
            P(),
            P(None, "gate"),
            P(),
            P(None, "gate"),
            P(None, None, None, "gate"),
            P(),
            P(),
            P(None, "gate"),
            P(),
            P(None, "gate"),
            P(None, None, None, "gate"),
            P(),
            P(),
        ),
        check_vma=False,
    )
```

profile of v0, /device:TPU:0, one launch (start us, length us, event | category | flops | bytes accessed | tf_op | source)
XLA Modules:
  0.0 1600.9 jit_solution(14914171004898042022)
XLA Ops:
  12.3 5.2 multiply_convert_fusion
  17.5 17.7 %fusion.64 = bf16[624,8,32,128]{3,1,2,0:T(8,128)(2,1)} fusion(f32[4096]{0:T(1024)S(1)} %bitcast.517, bf16[4992,128]{1,0:T(8,128)(2,1)} %get-tuple-element.765, f32[129,4096]{1,0:T(8,128)S(1)} %copy-done.10), kind=kOutput, calls=%fused_computation.106 | convolution fusion | flops 5275385856 | bytes 43237376 | tf_op jit(solution)/shard_map/dot_general | solution.py:31
  35.2 27.7 %copy.162 = bf16[624,8,32,128]{3,2,1,0:T(8,128)(2,1)} copy(bf16[624,8,32,128]{3,1,2,0:T(8,128)(2,1)} %fusion.64) | data formatting | bytes 81788928
  64.3 11.9 all_gather.21
  76.6 125.4 %while.75 = (s32[]{:T(128)}, f32[2432,32]{1,0:T(8,128)S(1)}, s32[13,384]{1,0:T(8,128)}, bf16[13,384,32,128]{3,2,1,0:T(8,128)(2,1)}, s32[13,384]{1,0:T(8,128)}, /*index=5*/bf16[2432,128]{1,0:T(8,128)(2,1)S(1)}, s32[]{:T(128)}) while((s32[]{:T(128)}, f32[2432,32]{1,0:T(8,128)S(1)}, s32[13,384]{1,0:T(8,128)}, ...), condition=%wide.region_2.3_spmd, body=%wide.region_0.2_spmd.sunk | while | flops 3160194 | bytes 3652693 | solution.py:168
  202.3 11.1 all_gather.22
  215.5 9.7 all_gather.23
  226.2 125.5 %while.76 = (s32[]{:T(128)}, f32[2432,32]{1,0:T(8,128)S(1)}, s32[13,384]{1,0:T(8,128)}, bf16[13,384,32,128]{3,2,1,0:T(8,128)(2,1)}, s32[13,384]{1,0:T(8,128)}, /*index=5*/bf16[2432,128]{1,0:T(8,128)(2,1)S(1)}, s32[]{:T(128)}) while((s32[]{:T(128)}, f32[2432,32]{1,0:T(8,128)S(1)}, s32[13,384]{1,0:T(8,128)}, ...), condition=%wide.region_5.6_spmd, body=%wide.region_3.5_spmd.sunk | while | flops 3160194 | bytes 3652693 | solution.py:168
  351.9 11.0 all_gather.24
  365.3 9.5 all_gather.25
  378.1 125.4 %while.77 = (s32[]{:T(128)}, f32[2432,32]{1,0:T(8,128)S(1)}, s32[13,384]{1,0:T(8,128)}, bf16[13,384,32,128]{3,2,1,0:T(8,128)(2,1)}, s32[13,384]{1,0:T(8,128)}, /*index=5*/bf16[2432,128]{1,0:T(8,128)(2,1)S(1)}, s32[]{:T(128)}) while((s32[]{:T(128)}, f32[2432,32]{1,0:T(8,128)S(1)}, s32[13,384]{1,0:T(8,128)}, ...), condition=%wide.region_8.9_spmd, body=%wide.region_6.8_spmd.sunk | while | flops 3160194 | bytes 3652693 | solution.py:168
  503.8 10.5 all_gather.26
  515.7 10.0 all_gather.27
  582.4 3.9 convert_reduce_fusion.1
  591.1 16.2 %psum.70 = f32[]{:T(128)} all-reduce(f32[]{:T(128)} %convert_reduce_fusion.13), channel_id=1, replica_groups=mesh['grp'=2,'edge'=4,'gate'=4] {'grp','edge'}, use_global_device_ids=true, to_apply=%region_23.24 | all-reduce | flops 1 | bytes 8 | tf_op jit(solution)/shard_map/psum | solution.py:176
  663.8 3.7 multiply_add_fusion.1
  673.1 27.9 %reduce-scatter.7.cloned.1.call-done = f32[2432,32]{0,1:T(8,128)} async-done(((f32[2432,128]{0,1:T(8,128)}), f32[2432,32]{0,1:T(8,128)}) %reduce-scatter.7.cloned.1.call-update) | async-done | bytes 311312 | tf_op jit(solution)/shard_map/reduce_scatter | solution.py:202
  702.4 129.0 %while.78 = (s32[]{:T(128)}, f32[2432,128]{1,0:T(8,128)S(1)}, s32[13,384]{1,0:T(8,128)}, bf16[13,384,32,128]{3,2,1,0:T(8,128)(2,1)}, s32[13,384]{1,0:T(8,128)}, /*index=5*/bf16[2432,32]{1,0:T(8,128)(2,1)S(1)}, s32[]{:T(128)}) while((s32[]{:T(128)}, f32[2432,128]{1,0:T(8,128)S(1)}, s32[13,384]{1,0:T(8,128)}, ...), condition=%wide.region_46.47_spmd, body=%wide.region_44.46_spmd.sunk | while | flops 3197058 | bytes 4021333 | solution.py:216
  835.9 29.0 %reduce-scatter.9.cloned.1.call-done = f32[2432,32]{0,1:T(8,128)} async-done(((f32[2432,128]{0,1:T(8,128)}), f32[2432,32]{0,1:T(8,128)}) %reduce-scatter.9.cloned.1.call-update) | async-done | bytes 311312 | tf_op jit(solution)/shard_map/reduce_scatter | solution.py:218
  878.2 21.2 %reduce-scatter.11.cloned.1.call-done = f32[2432,32]{0,1:T(8,128)} async-done(((f32[2432,128]{0,1:T(8,128)}), f32[2432,32]{0,1:T(8,128)}) %reduce-scatter.11.cloned.1.call-update) | async-done | bytes 311312 | tf_op jit(solution)/shard_map/reduce_scatter | solution.py:202
  900.8 115.1 %while.79 = (s32[]{:T(128)}, f32[2432,128]{1,0:T(8,128)S(1)}, s32[13,384]{1,0:T(8,128)}, bf16[13,384,32,128]{3,2,1,0:T(8,128)(2,1)}, s32[13,384]{1,0:T(8,128)}, /*index=5*/bf16[2432,32]{1,0:T(8,128)(2,1)S(1)}, s32[]{:T(128)}) while((s32[]{:T(128)}, f32[2432,128]{1,0:T(8,128)S(1)}, s32[13,384]{1,0:T(8,128)}, ...), condition=%wide.region_51.52_spmd, body=%wide.region_49.51_spmd.sunk | while | flops 3197058 | bytes 4021333 | solution.py:216
  1042.1 7.2 reduce-scatter.13.cloned.1.call-done
  1062.3 21.4 %reduce-scatter.15.cloned.1.call-done = f32[2432,32]{0,1:T(8,128)} async-done(((f32[2432,128]{0,1:T(8,128)}), f32[2432,32]{0,1:T(8,128)}) %reduce-scatter.15.cloned.1.call-update) | async-done | bytes 311312 | tf_op jit(solution)/shard_map/reduce_scatter | solution.py:202
  1087.5 292.9 %while.81 = (s32[]{:T(128)}, f32[128,4096]{1,0:T(8,128)}, f32[4096]{0:T(1024)}, f32[17,128]{1,0:T(8,128)}, bf16[13,384,128]{2,1,0:T(8,128)(2,1)}, /*index=5*/s32...) while((s32[]{:T(128)}, f32[128,4096]{1,0:T(8,128)}, ...), condition=%wide.region_63.64_spmd.clone, body=%wide.region_60.63_spmd.clone.sunk | while | flops 830408832 | bytes 21003968 | solution.py:263
  1088.3 3.7 gather_fusion.6
  1125.7 4.3 convolution_add_fusion.28
  1132.1 3.7 gather_fusion.6
  1148.3 4.3 convolution_add_fusion.28
  1171.0 4.3 convolution_add_fusion.28
  1193.6 4.3 convolution_add_fusion.28
  1216.3 4.3 convolution_add_fusion.28
  1222.7 3.7 gather_fusion.6
  1238.9 4.3 convolution_add_fusion.28
  1261.6 4.3 convolution_add_fusion.28
  1267.9 3.7 gather_fusion.6
  1284.2 4.3 convolution_add_fusion.28
  1290.6 3.7 gather_fusion.6
  1306.9 4.3 convolution_add_fusion.28
  1329.5 4.3 convolution_add_fusion.28
  1352.2 4.3 convolution_add_fusion.28
  1358.5 3.7 gather_fusion.6
  1374.8 4.3 convolution_add_fusion.28
  1385.1 115.5 %while.80 = (s32[]{:T(128)}, f32[2432,128]{1,0:T(8,128)S(1)}, s32[13,384]{1,0:T(8,128)}, bf16[13,384,32,128]{3,2,1,0:T(8,128)(2,1)}, s32[13,384]{1,0:T(8,128)}, /*index=5*/bf16[2432,32]{1,0:T(8,128)(2,1)S(1)}, s32[]{:T(128)}) while((s32[]{:T(128)}, f32[2432,128]{1,0:T(8,128)S(1)}, s32[13,384]{1,0:T(8,128)}, ...), condition=%wide.region_56.57_spmd, body=%wide.region_54.56_spmd.sunk | while | flops 3197058 | bytes 4021333 | solution.py:216
  1506.8 15.6 psum.76
  1527.5 5.0 reduce-scatter.17.cloned.1.call-done
  1534.3 29.9 %all-reduce.56 = (f32[]{:T(128)}, f32[16,32]{1,0:T(8,128)S(1)}, f32[17,128]{1,0:T(8,128)S(1)}, f32[257,12]{0,1:T(8,128)S(1)}) all-reduce(f32[]{:T(128)S(6)} %div.275, f32[16,32]{1,0:T(8,128)S(1)} %convolution_bitcast_fusion, f32[17,128]{1,0:T(8,128)S(1)} %psum.76, ...), channel_id=1, replica_groups=mesh['grp'=2,'edge'=4,'gate'=4] {'grp','edge'}, use_global_device_ids=true, to_apply=%region_24.25 | all-reduce | flops 5773 | bytes 46184 | tf_op jit(solution)/shard_map/psum | solution.py:273
  1567.9 9.4 psum.75
  1585.7 5.7 multiply_subtract_fusion
  (1513 shorter events, 1176.5 us)
Async XLA Ops:
  7.2 56.9 %copy-start = (bf16[2432,16]{0,1:T(8,128)(2,1)S(1)}, bf16[2432,16]{0,1:T(8,128)(2,1)}, u32[]{:S(2)}) copy-start(bf16[2432,16]{0,1:T(8,128)(2,1)} %param.41) | copy-start | bytes 233476
  7.2 693.8 %reduce-scatter.7.cloned.1.call-start = ((), (), s32[]{:S(2)}) async-start(), calls=%async_computation.6 | async-start | bytes 1556480 | tf_op jit(solution)/shard_map/reduce_scatter | solution.py:202
  8.2 217.4 %copy-start.147 = (bf16[2,129,3,32]{1,3,2,0:T(8,128)(2,1)}, bf16[2,129,3,32]{1,3,2,0:T(8,128)(2,1)S(1)}, u32[]{:S(2)}) copy-start(bf16[2,129,3,32]{1,3,2,0:T(8,128)(2,1)S(1)} %convert.7) | copy-start | bytes 148612
  35.1 27.7 %copy-start.254 = (s32[4992]{0:T(1024)S(1)}, s32[4992]{0:T(1024)}, u32[]{:S(2)}) copy-start(s32[4992]{0:T(1024)} %param.45) | copy-start | bytes 59908
  35.2 28.3 %copy-start.255 = (s32[4992]{0:T(1024)S(1)}, s32[4992]{0:T(1024)}, u32[]{:S(2)}) copy-start(s32[4992]{0:T(1024)} %param.44) | copy-start | bytes 59908
  35.2 28.9 %copy-start.252 = (f32[16,32]{1,0:T(8,128)S(1)}, f32[16,32]{1,0:T(8,128)}, u32[]{:S(2)}) copy-start(f32[16,32]{1,0:T(8,128)} %param.49) | copy-start | bytes 6148
  64.3 150.0 %copy-start.43 = (f32[2432,32]{0,1:T(8,128)}, f32[2432,32]{0,1:T(8,128)S(1)}, u32[]{:S(2)}) copy-start(f32[2432,32]{0,1:T(8,128)S(1)} %get-tuple-element.764) | copy-start | bytes 933892
  76.2 137.3 %copy-start.3 = (bf16[2432,128]{0,1:T(8,128)(2,1)}, bf16[2432,128]{0,1:T(8,128)(2,1)S(1)}, u32[]{:S(2)}) copy-start(bf16[2432,128]{0,1:T(8,128)(2,1)S(1)} %all_gather.21) | copy-start | bytes 1867780
  215.5 148.5 %copy-start.46 = (f32[2432,32]{0,1:T(8,128)}, f32[2432,32]{0,1:T(8,128)S(1)}, u32[]{:S(2)}) copy-start(f32[2432,32]{0,1:T(8,128)S(1)} %get-tuple-element.726) | copy-start | bytes 933892
  226.1 138.0 %copy-start.15 = (f32[2432,3,32]{0,2,1:T(8,128)}, f32[2432,3,32]{0,2,1:T(8,128)S(1)}, u32[]{:S(2)}) copy-start(f32[2432,3,32]{0,2,1:T(8,128)S(1)} %convolution_add_fusion.7) | copy-start | bytes 2801668
  351.7 12.1 copy-start.148
  503.8 10.8 copy-start.17
  503.8 10.8 copy-start.52
  514.6 11.1 copy-start.136
  515.7 11.2 copy-start.18
  526.9 9.7 copy-start.89
  526.9 10.1 copy-start.160
  529.8 52.5 %copy-start.178 = (f32[2432]{0:T(1024)}, f32[2432]{0:T(1024)S(1)}, u32[]{:S(2)}) copy-start(f32[2432]{0:T(1024)S(1)} %get-tuple-element.767) | copy-start | bytes 29188
  540.6 41.8 %copy-start.180 = (f32[2432]{0:T(1024)}, f32[2432]{0:T(1024)S(1)}, u32[]{:S(2)}) copy-start(f32[2432]{0:T(1024)S(1)} %get-tuple-element.769) | copy-start | bytes 29188
  541.9 40.4 %copy-start.273 = (f32[128]{0:T(128)}, f32[128]{0:T(128)S(1)}, u32[]{:S(2)}) copy-start(f32[128]{0:T(128)S(1)} %select_reduce_fusion.4) | copy-start | bytes 1540
  547.4 9.2 copy-start.154
  550.2 32.2 %copy-start.182 = (f32[2432]{0:T(1024)}, f32[2432]{0:T(1024)S(1)}, u32[]{:S(2)}) copy-start(f32[2432]{0:T(1024)S(1)} %get-tuple-element.771) | copy-start | bytes 29188
  551.9 30.4 %copy-start.275 = (f32[128]{0:T(128)}, f32[128]{0:T(128)S(1)}, u32[]{:S(2)}) copy-start(f32[128]{0:T(128)S(1)} %select_reduce_fusion.3) | copy-start | bytes 1540
  560.1 22.2 %copy-start.184 = (f32[2432]{0:T(1024)}, f32[2432]{0:T(1024)S(1)}, u32[]{:S(2)}) copy-start(f32[2432]{0:T(1024)S(1)} %get-tuple-element.773) | copy-start | bytes 29188
  561.5 20.9 %copy-start.277 = (f32[128]{0:T(128)}, f32[128]{0:T(128)S(1)}, u32[]{:S(2)}) copy-start(f32[128]{0:T(128)S(1)} %select_reduce_fusion.2) | copy-start | bytes 1540
  569.7 12.7 copy-start.186
  571.2 11.1 copy-start.279
  577.3 31.9 %copy-start.138 = (f32[128,128]{1,0:T(8,128)}, f32[128,128]{1,0:T(8,128)S(1)}, u32[]{:S(2)}) copy-start(f32[128,128]{1,0:T(8,128)S(1)} %get-tuple-element.706) | copy-start | bytes 196612
  577.3 11.2 copy-start.269
  577.3 11.2 copy-start.271
  581.4 27.8 %copy-start.264 = (f32[128,12]{0,1:T(8,128)S(1)}, f32[128,12]{0,1:T(8,128)}, u32[]{:S(2)}) copy-start(f32[128,12]{0,1:T(8,128)} %param.48) | copy-start | bytes 18436
  673.1 191.9 %reduce-scatter.9.cloned.1.call-start = ((), (), s32[]{:S(2)}) async-start(), calls=%async_computation.7 | async-start | bytes 1556480 | tf_op jit(solution)/shard_map/reduce_scatter | solution.py:218
  832.9 32.0 %copy-start.23 = (f32[2432,3,32]{0,2,1:T(8,128)S(1)}, f32[2432,3,32]{0,2,1:T(8,128)}, u32[]{:S(2)}) copy-start(f32[2432,3,32]{0,2,1:T(8,128)} %copy-done.22) | copy-start | bytes 2801668
  835.9 29.1 %copy-start.16 = (f32[2432,3,32]{0,2,1:T(8,128)S(1)}, f32[2432,3,32]{0,2,1:T(8,128)}, u32[]{:S(2)}) copy-start(f32[2432,3,32]{0,2,1:T(8,128)} %copy-done.15) | copy-start | bytes 2801668
  835.9 63.6 %reduce-scatter.11.cloned.1.call-start = ((), (), s32[]{:S(2)}) async-start(), calls=%async_computation.8 | async-start | bytes 1556480 | tf_op jit(solution)/shard_map/reduce_scatter | solution.py:202
  870.3 178.9 %reduce-scatter.13.cloned.1.call-start = ((), (), s32[]{:S(2)}) async-start(), calls=%async_computation.9 | async-start | bytes 1556480 | tf_op jit(solution)/shard_map/reduce_scatter | solution.py:218
  1020.2 63.5 %reduce-scatter.15.cloned.1.call-start = ((), (), s32[]{:S(2)}) async-start(), calls=%async_computation.10 | async-start | bytes 1556480 | tf_op jit(solution)/shard_map/reduce_scatter | solution.py:202
  1038.6 10.7 copy-start.21
  1040.1 9.2 copy-start.14
  1040.1 9.2 copy-start.30
  1054.7 467.8 %all-reduce.60.cloned.1.call-start = ((), (), s32[]{:S(2)}) async-start(), calls=%async_computation.12 | async-start | bytes 6455296 | tf_op jit(solution)/shard_map/psum | solution.py:273
  1385.0 147.5 %reduce-scatter.17.cloned.1.call-start = ((), (), s32[]{:S(2)}) async-start(), calls=%async_computation.11 | async-start | bytes 1556480 | tf_op jit(solution)/shard_map/reduce_scatter | solution.py:218
  1524.4 9.3 copy-start.150
  1524.4 55.6 %copy-start.215 = (f32[257,12]{0,1:T(8,128)S(1)}, f32[257,12]{0,1:T(8,128)}, u32[]{:S(2)}) copy-start(f32[257,12]{0,1:T(8,128)} %param.54) | copy-start | bytes 37012
  1524.4 57.1 %copy-start.42 = (f32[385,512]{1,0:T(8,128)S(1)}, f32[385,512]{1,0:T(8,128)}, u32[]{:S(2)}) copy-start(f32[385,512]{1,0:T(8,128)} %get-tuple-element.642) | copy-start | bytes 2365444
  1524.4 57.1 %copy-start.149 = (f32[385,512]{1,0:T(8,128)S(1)}, f32[385,512]{1,0:T(8,128)}, u32[]{:S(2)}) copy-start(f32[385,512]{1,0:T(8,128)} %param.65) | copy-start | bytes 2365444
  1527.5 54.0 %copy-start.2 = (f32[385,512]{1,0:T(8,128)S(1)}, f32[385,512]{1,0:T(8,128)}, u32[]{:S(2)}) copy-start(f32[385,512]{1,0:T(8,128)} %param.53) | copy-start | bytes 2365444
  1532.4 52.3 %copy-start.135 = (f32[2,129,3,32]{1,3,2,0:T(8,128)S(1)}, f32[2,129,3,32]{1,3,2,0:T(8,128)}, u32[]{:S(2)}) copy-start(f32[2,129,3,32]{1,3,2,0:T(8,128)} %param.52) | copy-start | bytes 297220
  (262 other events, 786.8 us)
Sparse Core Ops, SparseCore 0:
  673.2 27.7 reduce-scatter.6
  836.0 28.9 reduce-scatter.8
  870.5 28.9 reduce-scatter.10
  1020.3 28.9 reduce-scatter.12
  1054.8 28.9 reduce-scatter.14
  1385.1 79.7 all-reduce.59
  1503.3 29.1 reduce-scatter.16
where the time goes:
time: 1630 us; the launch traced here: 1600 us
  matrix products  553 us (34%)
  other arithmetic  421 us (26%)
  local copies, waits for them, and re-layouts  339 us (21%)
  blocking collectives  145 us (9%)
  waiting for transfers between devices  112 us (7%)
  between operations  27.4 us (2%)
    dot_general x39, matrix products, send_one_block(): jnp.einsum('eoi,ei->eo', mats, hidden_full[src_rows], preferred_element_t...  140 us
    scatter-add x39, other arithmetic, return_one_block(): jax.ops.segment_sum(parts, src_rows, num_segments=nodes)  125 us
    scatter-add x39, other arithmetic, send_one_block(): jax.ops.segment_sum(parts, tgt_rows, num_segments=nodes)  120 us
    dot_general x39, matrix products, return_one_block(): jnp.einsum('eoi,eo->ei', mats, d_msg_low[tgt_rows], preferred_element_typ...  119 us
    dot_general x46, matrix products, tdot(): lax.dot_general(left, right, (((0,), (0,)), ((), ())), precision=HIGH if...  88.2 us
    dot_general x87, matrix products, fdot(): jnp.dot(left, right, precision=HIGH, preferred_element_type=jnp.float32)  83.7 us
    reduce_scatter x3, waiting for transfers between devices, on_device(): lax.psum_scatter(ndot(d_gin_low, gru_low[0]), 'gate', scatter_dimension=1...  70.5 us
    dynamic_slice x91, local copies, waits for them, and re-layouts, on_device(): lax.scan(send_one_block, jnp.zeros((nodes, width), jnp.float32), block_data)  67.6 us
  transfers between devices with their start and end apart: 7, of which 6 were waited for; matrix products, arithmetic and copies ran while one was open for 10% of the time, Pallas kernels for 0%

commit v1 on v0

v1 whole, which is shorter than its diff:
```python
import functools
import math

import jax
import jax.numpy as jnp
from jax import lax
from jax.experimental import pallas as pl
from jax.experimental.pallas import tpu as pltpu
from jax.sharding import PartitionSpec as P

H = 128
EDGE_HID = 128
NT = 12
BONDS = 4
STEPS = 3
SET_STEPS = 6
EIN = 16
BLK = 256
FEAT = 32

CLIP = 0.01
BETA_ONE = 0.9
BETA_TWO = 0.999
EPSILON = 1e-08
DECAY = 0.01
RATES = (0.1, 0.05, 0.005, 0.02, 0.02, 0.02)

F32 = jnp.float32
BF = jnp.bfloat16
VMEM_LIMIT = 60 << 20


def up(value, multiple):
    return -(-value // multiple) * multiple


def dot(left, right):
    return jnp.dot(left, right, preferred_element_type=F32)


def dot_nt(left, right):
    return lax.dot_general(
        left, right, (((1,), (1,)), ((), ())), preferred_element_type=F32
    )


def dot_tn(left, right):
    return lax.dot_general(
        left, right, (((0,), (0,)), ((), ())), preferred_element_type=F32
    )


def split2(value):
    high = value.astype(BF)
    return high, (value - high.astype(F32)).astype(BF)


def split3(value):
    high = value.astype(BF)
    rest = value - high.astype(F32)
    mid = rest.astype(BF)
    return high, mid, (rest - mid.astype(F32)).astype(BF)


def wide(product, left, right):
    lh, ll = split2(left)
    rh, rl = split2(right)
    return product(lh, rh) + (product(lh, rl) + product(ll, rh))


def half_wide(product, left, right):
    lh, lm, ll = split3(left)
    return product(lh, right) + (product(lm, right) + product(ll, right))


def sigmoid(value):
    return jax.nn.sigmoid(value)


def ceil_blocks(value):
    return lax.div(value + (BLK - 1), BLK)


def node_hit(row, block):
    ids = lax.broadcasted_iota(jnp.int32, (BLK, BLK), 0) + block * BLK
    return jnp.where(row == ids, 1.0, 0.0).astype(BF)


def at(block):
    return pl.ds(pl.multiple_of(block * BLK, BLK), BLK)


def prep_kernel(place, mol, src2d, data, first3, scal, pre, eh_t, eh, feat, idx, comp, *, nodes, gates, eblocks):
    mine = place[0]
    mols = lax.broadcasted_iota(jnp.int32, (H, 1), 0)
    row = mol[...]
    size = jnp.sum(jnp.where(row == mols, 1.0, 0.0), axis=1, keepdims=True)
    start = jnp.sum(jnp.where(row < mols, 1.0, 0.0), axis=1, keepdims=True)
    middle = 2.0 * start + size
    owner = jnp.zeros((H, 1), F32)
    for step in range(1, gates):
        owner = owner + jnp.where(middle * gates >= 2.0 * nodes * step, 1.0, 0.0)
    before = jnp.where(owner < mine.astype(F32), 1.0, 0.0)
    until = jnp.where(owner <= mine.astype(F32), 1.0, 0.0)
    node_lo = jnp.sum(size * before).astype(jnp.int32)
    node_hi = jnp.sum(size * until).astype(jnp.int32)
    scal[0] = node_lo
    scal[1] = node_hi
    scal[2] = jnp.sum(before).astype(jnp.int32)
    scal[3] = jnp.sum(until).astype(jnp.int32)
    ids = src2d[...]
    mask = jnp.where((ids >= node_lo) & (ids < node_hi), 1.0, 0.0)
    lower = lax.broadcasted_iota(jnp.int32, (BLK, BLK), 0)
    upper = lax.broadcasted_iota(jnp.int32, (BLK, BLK), 1)
    prefix = dot(mask.astype(BF), jnp.where(lower <= upper, 1.0, 0.0).astype(BF))
    totals = jnp.sum(mask, axis=1, keepdims=True)
    rows = lax.broadcasted_iota(jnp.int32, totals.shape, 0)
    slots = lax.broadcasted_iota(jnp.int32, (BLK, BLK), 0).astype(F32)
    for block in range(eblocks):
        offset = jnp.sum(jnp.where(rows < block, totals, 0.0)).astype(jnp.int32)
        hit = jnp.where(prefix[block : block + 1] - 1.0 == slots, mask[block : block + 1], 0.0)
        comp[pl.ds(offset, BLK), :] = dot(hit.astype(BF), data[block * BLK : (block + 1) * BLK, :])
    count = jnp.sum(totals).astype(jnp.int32)
    comp[pl.ds(count, BLK), :] = jnp.zeros((BLK, H), F32)
    scal[4] = count

    def each(block, carry):
        part = comp[at(block), :]
        part_t = part.T
        low = part_t[0:FEAT].astype(BF)
        feat[:, at(block)] = low
        source = 16.0 * part_t[17:18] + part_t[18:19] - 1.0
        target = 16.0 * part_t[19:20] + part_t[20:21] - 1.0
        idx[0:1, at(block)] = source.astype(jnp.int32)
        idx[1:2, at(block)] = target.astype(jnp.int32)
        three = dot(first3[...], low)
        value = three[0:H] + (three[H : 2 * H] + three[2 * H : 3 * H])
        pre[:, at(block)] = value
        hidden = value * sigmoid(value)
        eh_t[:, at(block)] = hidden.astype(BF)
        eh[at(block), :] = hidden.T.astype(BF)
        return carry

    lax.fori_loop(0, ceil_blocks(count), each, 0)


def prep(place, mol, src2d, data, first3, nodes, gates):
    edges = data.shape[0]
    return pl.pallas_call(
        functools.partial(prep_kernel, nodes=nodes, gates=gates, eblocks=edges // BLK),
        out_shape=(
            jax.ShapeDtypeStruct((8,), jnp.int32),
            jax.ShapeDtypeStruct((H, edges), F32),
            jax.ShapeDtypeStruct((H, edges), BF),
            jax.ShapeDtypeStruct((edges, H), BF),
            jax.ShapeDtypeStruct((FEAT, edges), BF),
            jax.ShapeDtypeStruct((8, edges), jnp.int32),
        ),
        in_specs=[pl.BlockSpec(memory_space=pltpu.SMEM)] + [pl.BlockSpec(memory_space=pltpu.VMEM)] * 4,
        out_specs=[pl.BlockSpec(memory_space=pltpu.SMEM)] + [pl.BlockSpec(memory_space=pltpu.VMEM)] * 5,
        scratch_shapes=[pltpu.VMEM((edges + BLK, H), F32)],
        compiler_params=pltpu.CompilerParams(vmem_limit_bytes=VMEM_LIMIT),
        name="prep",
    )(place, mol, src2d, data, first3)


def matrices(second, bias, chunk, low):
    width = bias.shape[2]
    flat = dot(second[chunk], low)
    out = []
    for column in range(width):
        part = flat[column * H : (column + 1) * H] + bias[chunk][:, column : column + 1]
        out.append(part.astype(BF).astype(F32))
    return out


def gru_parts(gru, gru_bias, message, hidden):
    gate_in = dot(gru[0], message) + gru_bias[0]
    gate_hid = dot(gru[1], hidden) + gru_bias[1]
    reset = sigmoid(gate_in[0:H] + gate_hid[0:H])
    update = sigmoid(gate_in[H : 2 * H] + gate_hid[H : 2 * H])
    last = gate_hid[2 * H : 3 * H]
    fresh = jnp.tanh(gate_in[2 * H : 3 * H] + reset * last)
    return reset, update, fresh, last


def forward_kernel(scal, nf_t, embed, second, bias, gru, gru_bias, eh_t, idx, hid, msg, state, near, total, part, *, chunks):
    first_block = lax.div(scal[0], BLK)
    last_block = ceil_blocks(scal[1])
    edge_blocks = ceil_blocks(scal[4])
    width = bias.shape[2]

    def begin(block, carry):
        value = dot(embed[...], nf_t[:, at(block)])
        state[0, :, at(block)] = value
        hid[0, :, at(block)] = value.astype(BF)
        return carry

    lax.fori_loop(first_block, last_block, begin, 0)
    for step in range(STEPS):

        def clear(block, carry):
            total[:, at(block)] = jnp.zeros((H, BLK), F32)
            return carry

        lax.fori_loop(first_block, last_block, clear, 0)

        def edge_block(block, carry):
            source = idx[0:1, at(block)]
            target = idx[1:2, at(block)]

            def gather(node, acc):
                return acc + dot(hid[step, :, at(node)], node_hit(source, node))

            rows = lax.fori_loop(first_block, last_block, gather, jnp.zeros((H, BLK), F32))
            near[step, :, at(block)] = rows.astype(BF)
            low = eh_t[:, at(block)]

            def chunk_loop(chunk, carry):
                mats = matrices(second, bias, chunk, low)
                outs = [jnp.sum(mat * rows, axis=0, keepdims=True) for mat in mats]
                part[pl.ds(pl.multiple_of(chunk * width, width), width), :] = jnp.concatenate(outs, axis=0)
                return carry

            lax.fori_loop(0, chunks, chunk_loop, 0)
            pair = jnp.concatenate(split2(part[...]), axis=0)

            def scatter(node, carry):
                both = dot_nt(pair, node_hit(target, node))
                total[:, at(node)] += both[0:H] + both[H : 2 * H]
                return carry

            lax.fori_loop(first_block, last_block, scatter, 0)
            return carry

        lax.fori_loop(0, edge_blocks, edge_block, 0)

        def cell(block, carry):
            message = total[:, at(block)].astype(BF)
            msg[step, :, at(block)] = message
            old = state[step, :, at(block)]
            reset, update, fresh, last = gru_parts(gru, gru_bias, message, hid[step, :, at(block)])
            new = (1.0 - update) * fresh + update * old
            hid[step + 1, :, at(block)] = new.astype(BF)
            if step + 1 < STEPS:
                state[step + 1, :, at(block)] = new
            return carry

        lax.fori_loop(first_block, last_block, cell, 0)


def forward(scal, nf_t, embed, second, bias, gru, gru_bias, eh_t, idx):
    nodes = nf_t.shape[1]
    edges = eh_t.shape[1]
    chunks = second.shape[0]
    return pl.pallas_call(
        functools.partial(forward_kernel, chunks=chunks),
        out_shape=(
            jax.ShapeDtypeStruct((STEPS + 1, H, nodes), BF),
            jax.ShapeDtypeStruct((STEPS, H, nodes), BF),
            jax.ShapeDtypeStruct((STEPS, H, nodes), F32),
            jax.ShapeDtypeStruct((STEPS, H, edges), BF),
        ),
        in_specs=[pl.BlockSpec(memory_space=pltpu.SMEM)] + [pl.BlockSpec(memory_space=pltpu.VMEM)] * 8,
        out_specs=[pl.BlockSpec(memory_space=pltpu.VMEM)] * 4,
        scratch_shapes=[pltpu.VMEM((H, nodes), F32), pltpu.VMEM((H, BLK), F32)],
        compiler_params=pltpu.CompilerParams(vmem_limit_bytes=VMEM_LIMIT),
        name="forward",
    )(scal, nf_t, embed, second, bias, gru, gru_bias, eh_t, idx)


def readout_kernel(scal, inverse, final, mol, lstm, head, present, target, loss, d_final, d_lstm, d_head, score, weight, slope, before):
    first_block = lax.div(scal[0], BLK)
    last_block = ceil_blocks(scal[1])
    mols = lax.broadcasted_iota(jnp.int32, (H, 1), 0)
    owned = jnp.where((mols >= scal[2]) & (mols < scal[3]), 1.0, 0.0)
    by_query = lstm[0:H, :] + lstm[2 * H : 3 * H, :]
    by_summary = lstm[H : 2 * H, :]
    lstm_bias = lstm[3 * H : 3 * H + 1, :]
    zero = jnp.zeros((H, H), F32)
    query, summary, cell = zero, zero, zero
    kept = []
    for rounds in range(SET_STEPS):
        gates = jnp.broadcast_to(lstm_bias, (H, 4 * H))
        if rounds:
            gates = gates + wide(dot, query, by_query) + wide(dot, summary, by_summary)
        enter = sigmoid(gates[:, 0:H])
        forget = sigmoid(gates[:, H : 2 * H])
        fresh = jnp.tanh(gates[:, 2 * H : 3 * H])
        leave = sigmoid(gates[:, 3 * H : 4 * H])
        old_cell, old_query, old_summary = cell, query, summary
        cell = forget * cell + enter * fresh
        bent = jnp.tanh(cell)
        query = leave * bent
        stack = jnp.concatenate(split3(query), axis=0)

        def scores(block, peak):
            three = dot(stack, final[:, at(block)])
            value = three[0:H] + (three[H : 2 * H] + three[2 * H : 3 * H])
            value = jnp.where(mol[:, at(block)] == mols, value, -1e30)
            score[:, at(block)] = value
            return jnp.maximum(peak, jnp.max(value, axis=1, keepdims=True))

        peak = lax.fori_loop(first_block, last_block, scores, jnp.full((H, 1), -1e30, F32))

        def powers(block, sums):
            value = jnp.where(mol[:, at(block)] == mols, jnp.exp(score[:, at(block)] - peak), 0.0)
            score[:, at(block)] = value
            return sums + jnp.sum(value, axis=1, keepdims=True)

        sums = lax.fori_loop(first_block, last_block, powers, jnp.zeros((H, 1), F32))
        sums = jnp.where(sums > 0.0, sums, 1.0)

        def gather(block, acc):
            value = score[:, at(block)] / sums
            weight[rounds, :, at(block)] = value
            three = dot_nt(jnp.concatenate(split3(value), axis=0), final[:, at(block)])
            return acc + (three[0:H] + (three[H : 2 * H] + three[2 * H : 3 * H]))

        summary = lax.fori_loop(first_block, last_block, gather, zero)
        kept.append((enter, forget, fresh, leave, bent, old_cell, old_query, old_summary, query))
    head_query = head[0:H, :]
    head_summary = head[H : 2 * H, :]
    guess = wide(dot, query, head_query) + wide(dot, summary, head_summary) + head[2 * H : 2 * H + 1, :]
    gap = guess - target[...]
    seen = present[...] * owned
    loss[...] = jnp.broadcast_to(jnp.sum(seen * gap * gap), (8, H)) * inverse[0]
    d_guess = (2.0 * inverse[0]) * seen * gap
    d_head[0:H, :] = wide(dot, query.T, d_guess)
    d_head[H : 2 * H, :] = wide(dot, summary.T, d_guess)
    d_head[2 * H : 2 * H + 8, :] = jnp.broadcast_to(jnp.sum(d_guess, axis=0, keepdims=True), (8, H))
    d_query = wide(dot_nt, d_guess, head_query)
    d_summary = wide(dot_nt, d_guess, head_summary)
    d_cell = zero
    d_bias = jnp.zeros((1, 4 * H), F32)

    def clear(block, carry):
        d_final[:, at(block)] = jnp.zeros((H, BLK), F32)
        return carry

    lax.fori_loop(first_block, last_block, clear, 0)
    for rounds in reversed(range(SET_STEPS)):
        enter, forget, fresh, leave, bent, old_cell, old_query, old_summary, query = kept[rounds]
        stack = jnp.concatenate(split3(d_summary), axis=0)

        def products(block, acc):
            three = dot(stack, final[:, at(block)])
            value = three[0:H] + (three[H : 2 * H] + three[2 * H : 3 * H])
            score[:, at(block)] = value
            return acc + jnp.sum(value * weight[rounds, :, at(block)], axis=1, keepdims=True)

        mean = lax.fori_loop(first_block, last_block, products, jnp.zeros((H, 1), F32))
        query_t = query.T
        d_summary_t = d_summary.T

        def spread(block, acc):
            share = weight[rounds, :, at(block)]
            d_score = share * (score[:, at(block)] - mean)
            d_final[:, at(block)] += wide(dot, query_t, d_score) + wide(dot, d_summary_t, share)
            three = dot_nt(jnp.concatenate(split3(d_score), axis=0), final[:, at(block)])
            return acc + (three[0:H] + (three[H : 2 * H] + three[2 * H : 3 * H]))

        d_query = lax.fori_loop(first_block, last_block, spread, d_query)
        d_leave = d_query * bent
        d_cell = d_cell + d_query * leave * (1.0 - bent * bent)
        d_gates = jnp.concatenate(
            [
                d_cell * fresh * enter * (1.0 - enter),
                d_cell * old_cell * forget * (1.0 - forget),
                d_cell * enter * (1.0 - fresh * fresh),
                d_leave * leave * (1.0 - leave),
            ],
            axis=1,
        )
        d_cell = d_cell * forget
        d_bias = d_bias + jnp.sum(d_gates, axis=0, keepdims=True)
        if rounds:
            slope[rounds - 1] = d_gates
            before[0, :, (rounds - 1) * H : rounds * H] = old_query.T
            before[1, :, (rounds - 1) * H : rounds * H] = old_summary.T
            d_query = wide(dot_nt, d_gates, by_query)
            d_summary = wide(dot_nt, d_gates, by_summary)
    slopes = slope[...].reshape((SET_STEPS - 1) * H, 4 * H)
    d_by_query = wide(dot, before[0], slopes)
    d_lstm[0:H, :] = d_by_query
    d_lstm[H : 2 * H, :] = wide(dot, before[1], slopes)
    d_lstm[2 * H : 3 * H, :] = d_by_query
    d_lstm[3 * H : 3 * H + 8, :] = jnp.broadcast_to(d_bias, (8, 4 * H))


def readout(scal, inverse, final, mol, lstm, head, present, target):
    nodes = final.shape[1]
    return pl.pallas_call(
        readout_kernel,
        out_shape=(
            jax.ShapeDtypeStruct((8, H), F32),
            jax.ShapeDtypeStruct((H, nodes), F32),
            jax.ShapeDtypeStruct((3 * H + 8, 4 * H), F32),
            jax.ShapeDtypeStruct((2 * H + 8, H), F32),
        ),
        in_specs=[pl.BlockSpec(memory_space=pltpu.SMEM)] * 2 + [pl.BlockSpec(memory_space=pltpu.VMEM)] * 6,
        out_specs=[pl.BlockSpec(memory_space=pltpu.VMEM)] * 4,
        scratch_shapes=[
            pltpu.VMEM((H, nodes), F32),
            pltpu.VMEM((SET_STEPS, H, nodes), F32),
            pltpu.VMEM((SET_STEPS - 1, H, 4 * H), F32),
            pltpu.VMEM((2, H, (SET_STEPS - 1) * H), F32),
        ],
        compiler_params=pltpu.CompilerParams(vmem_limit_bytes=VMEM_LIMIT),
        name="readout",
    )(scal, inverse, final, mol, lstm, head, present, target)


def backward_kernel(scal, nf_t, second, bias, gru, gru_bias, eh_t, idx, hid, msg, state, d_final, far, d_gru, d_embed, grad, low_msg, part, *, chunks):
    first_block = lax.div(scal[0], BLK)
    last_block = ceil_blocks(scal[1])
    edge_blocks = ceil_blocks(scal[4])
    width = bias.shape[2]
    d_gru[...] = jnp.zeros(d_gru.shape, F32)
    d_embed[...] = jnp.zeros(d_embed.shape, F32)
    ones = jnp.ones((16, BLK), BF)

    def begin(block, carry):
        grad[:, at(block)] = d_final[:, at(block)]
        return carry

    lax.fori_loop(first_block, last_block, begin, 0)
    for step in reversed(range(STEPS)):

        def cell(block, carry):
            message = msg[step, :, at(block)]
            hidden = hid[step, :, at(block)]
            old = state[step, :, at(block)]
            reset, update, fresh, last = gru_parts(gru, gru_bias, message, hidden)
            value = grad[:, at(block)]
            d_fresh = value * (1.0 - update) * (1.0 - fresh * fresh)
            d_update = value * (old - fresh) * update * (1.0 - update)
            d_reset = d_fresh * last * reset * (1.0 - reset)
            d_in = jnp.concatenate([d_reset, d_update, d_fresh], axis=0).astype(BF)
            d_hid = jnp.concatenate([d_reset, d_update, d_fresh * reset], axis=0).astype(BF)
            d_gru[0] += dot_nt(jnp.concatenate([message, ones], axis=0), d_in)
            d_gru[1] += dot_nt(jnp.concatenate([hidden, ones], axis=0), d_hid)
            low_msg[:, at(block)] = dot_tn(gru[0], d_in).astype(BF)
            grad[:, at(block)] = value * update + dot_tn(gru[1], d_hid)
            return carry

        lax.fori_loop(first_block, last_block, cell, 0)

        def edge_block(block, carry):
            source = idx[0:1, at(block)]
            target = idx[1:2, at(block)]

            def gather(node, acc):
                return acc + dot(low_msg[:, at(node)], node_hit(target, node))

            rows = lax.fori_loop(first_block, last_block, gather, jnp.zeros((H, BLK), F32))
            far[step, :, at(block)] = rows.astype(BF)
            part[...] = rows
            low = eh_t[:, at(block)]

            def chunk_loop(chunk, acc):
                mats = matrices(second, bias, chunk, low)
                scale = part[pl.ds(pl.multiple_of(chunk * width, width), width), :]
                for column in range(width):
                    acc = acc + mats[column] * scale[column : column + 1]
                return acc

            back = lax.fori_loop(0, chunks, chunk_loop, jnp.zeros((H, BLK), F32))
            pair = jnp.concatenate(split2(back), axis=0)

            def scatter(node, carry):
                both = dot_nt(pair, node_hit(source, node))
                grad[:, at(node)] += both[0:H] + both[H : 2 * H]
                return carry

            lax.fori_loop(first_block, last_block, scatter, 0)
            return carry

        lax.fori_loop(0, edge_blocks, edge_block, 0)

    def finish(block, carry):
        d_embed[...] += dot_nt(nf_t[:, at(block)], grad[:, at(block)].astype(BF))
        return carry

    lax.fori_loop(first_block, last_block, finish, 0)


def backward(scal, nf_t, second, bias, gru, gru_bias, eh_t, idx, hid, msg, state, d_final):
    nodes = nf_t.shape[1]
    edges = eh_t.shape[1]
    return pl.pallas_call(
        functools.partial(backward_kernel, chunks=second.shape[0]),
        out_shape=(
            jax.ShapeDtypeStruct((STEPS, H, edges), BF),
            jax.ShapeDtypeStruct((2, H + 16, 3 * H), F32),
            jax.ShapeDtypeStruct((16, H), F32),
        ),
        in_specs=[pl.BlockSpec(memory_space=pltpu.SMEM)] + [pl.BlockSpec(memory_space=pltpu.VMEM)] * 11,
        out_specs=[pl.BlockSpec(memory_space=pltpu.VMEM)] * 3,
        scratch_shapes=[pltpu.VMEM((H, nodes), F32), pltpu.VMEM((H, nodes), BF), pltpu.VMEM((H, BLK), F32)],
        compiler_params=pltpu.CompilerParams(vmem_limit_bytes=VMEM_LIMIT),
        name="backward",
    )(scal, nf_t, second, bias, gru, gru_bias, eh_t, idx, hid, msg, state, d_final)


def final_kernel(scal, second, near, far, eh, pre, feat, d_second, d_bias, d_first, d_pre, *, chunks, group):
    chunk = pl.program_id(0)
    edge_blocks = ceil_blocks(scal[4])
    width = H // chunks

    @pl.when(chunk == 0)
    def _():
        d_bias[...] = jnp.zeros(d_bias.shape, F32)
        d_first[...] = jnp.zeros(d_first.shape, F32)

        def clear(block, carry):
            d_pre[:, at(block)] = jnp.zeros((H, BLK), F32)
            for step in range(STEPS):
                d_bias[...] += dot_nt(far[step, :, at(block)], near[step, :, at(block)])
            return carry

        lax.fori_loop(0, edge_blocks, clear, 0)

    d_second[...] = jnp.zeros(d_second.shape, F32)

    def edge_block(block, carry):
        sides = [near[step, :, at(block)].astype(F32) for step in range(STEPS)]
        tops = [
            far[step, pl.ds(pl.multiple_of(chunk * width, width), width), at(block)].astype(F32)
            for step in range(STEPS)
        ]
        low = eh[at(block), :]
        acc = jnp.zeros((H, BLK), F32)
        for piece in range(width // group):
            mats = []
            for column in range(piece * group, (piece + 1) * group):
                value = sides[0] * tops[0][column : column + 1]
                for step in range(1, STEPS):
                    value = value + sides[step] * tops[step][column : column + 1]
                mats.append(value.astype(BF))
            flat = jnp.concatenate(mats, axis=0)
            rows = slice(piece * group * H, (piece + 1) * group * H)
            d_second[0, rows, :] += dot(flat, low)
            acc = acc + dot_tn(second[0, rows, :], flat)
        d_pre[:, at(block)] += acc
        return carry

    lax.fori_loop(0, edge_blocks, edge_block, 0)

    @pl.when(chunk == chunks - 1)
    def _():
        def close(block, carry):
            value = pre[:, at(block)]
            sig = sigmoid(value)
            slope = d_pre[:, at(block)] * sig * (1.0 + value * (1.0 - sig))
            for piece in split3(slope):
                d_first[...] += dot_nt(feat[:, at(block)], piece)
            return carry

        lax.fori_loop(0, edge_blocks, close, 0)


def edge_grads(scal, second, near, far, eh, pre, feat):
    chunks, rows, _ = second.shape
    edges = eh.shape[0]
    whole = pl.BlockSpec(memory_space=pltpu.VMEM)
    return pl.pallas_call(
        functools.partial(final_kernel, chunks=chunks, group=8),
        out_shape=(
            jax.ShapeDtypeStruct((chunks, rows, H), F32),
            jax.ShapeDtypeStruct((H, H), F32),
            jax.ShapeDtypeStruct((FEAT, H), F32),
        ),
        grid=(chunks,),
        in_specs=[
            pl.BlockSpec(memory_space=pltpu.SMEM),
            pl.BlockSpec((1, rows, H), lambda chunk: (chunk, 0, 0)),
            whole,
            whole,
            whole,
            whole,
            whole,
        ],
        out_specs=[
            pl.BlockSpec((1, rows, H), lambda chunk: (chunk, 0, 0)),
            pl.BlockSpec((H, H), lambda chunk: (0, 0)),
            pl.BlockSpec((FEAT, H), lambda chunk: (0, 0)),
        ],
        scratch_shapes=[pltpu.VMEM((H, edges), F32)],
        compiler_params=pltpu.CompilerParams(vmem_limit_bytes=VMEM_LIMIT),
        name="edge_grads",
    )(scal, second, near, far, eh, pre, feat)


def exact3(value):
    high = lax.reduce_precision(value, 8, 7)
    mid = lax.reduce_precision(value - high, 8, 7)
    low = lax.reduce_precision(value - high - mid, 8, 7)
    return jnp.stack([high, mid, low]).astype(BF)


def pack_rows(arrays, rows):
    flat = [array.reshape(-1, H) if array.size % H == 0 else None for array in arrays]
    out = []
    for array, done in zip(arrays, flat):
        if done is None:
            line = array.reshape(-1)
            done = jnp.pad(line, (0, up(line.size, H) - line.size)).reshape(-1, H)
        out.append(done)
    joined = jnp.concatenate(out, axis=0)
    return jnp.pad(joined, ((0, rows - joined.shape[0]), (0, 0)))


def adamw(weight, grad, mom, var, rate, count):
    mom_new = BETA_ONE * mom + (1.0 - BETA_ONE) * grad
    var_new = BETA_TWO * var + (1.0 - BETA_TWO) * grad * grad
    mom_hat = mom_new / (1.0 - BETA_ONE**count)
    var_hat = var_new / (1.0 - BETA_TWO**count)
    return (
        weight - rate * (mom_hat / (jnp.sqrt(var_hat) + EPSILON) + DECAY * weight),
        mom_new,
        var_new,
    )


def local_part(
    place, node_feat, dist_feat, bond, source, target_node, mol_id, present, target, inverse,
    gates, embed_t, second, bias, gru, gru_bias, edge_first, set_lstm, head_weight,
):
    nodes = node_feat.shape[0]
    edges = source.shape[0]
    mols = target.shape[0]
    wide_nodes = up(nodes, BLK)
    wide_edges = up(edges, BLK)
    one_hot = (bond[:, None] == jnp.arange(BONDS)[None, :]).astype(BF)
    src_one = source + 1
    tgt_one = target_node + 1
    index = jnp.stack([src_one >> 4, src_one & 15, tgt_one >> 4, tgt_one & 15], axis=1).astype(BF)
    data = jnp.concatenate([one_hot, dist_feat, jnp.ones((edges, 1), BF), index], axis=1)
    data = jnp.pad(data, ((0, wide_edges - edges), (0, H - data.shape[1])))
    src2d = jnp.pad(source, (0, wide_edges - edges), constant_values=-1).reshape(-1, BLK)
    src2d = jnp.pad(src2d, ((0, up(src2d.shape[0], 16) - src2d.shape[0]), (0, 0)), constant_values=-1)
    mol = jnp.pad(mol_id, (0, wide_nodes - nodes), constant_values=1 << 20).reshape(1, wide_nodes)
    nf_t = jnp.pad(node_feat.T, ((0, 0), (0, wide_nodes - nodes)))
    first_t = jnp.pad(edge_first.T, ((0, 0), (0, FEAT - EIN - 1)))
    first3 = exact3(first_t).reshape(3 * H, FEAT)
    scal, pre, eh_t, eh, feat, idx = prep(place, mol, src2d, data, first3, nodes, gates)
    hid, msg, state, near = forward(scal, nf_t, embed_t, second, bias, gru, gru_bias, eh_t, idx)
    lstm = jnp.pad(set_lstm, ((0, 7), (0, 0)))
    head = jnp.pad(head_weight, ((0, 7), (0, H - NT)))
    loss, d_final, d_lstm, d_head = readout(
        scal, inverse, hid[STEPS], mol, lstm, head,
        jnp.pad(present, ((0, H - mols), (0, H - NT))), jnp.pad(target, ((0, H - mols), (0, H - NT))),
    )
    far, d_gru, d_embed = backward(
        scal, nf_t, second, bias, gru, gru_bias, eh_t, idx, hid, msg, state, d_final
    )
    d_second, d_bias, d_first = edge_grads(scal, second, near, far, eh, pre, feat)
    return (
        loss[0, 0], d_lstm[: 3 * H + 1], d_head[: 2 * H + 1, :NT], d_gru[:, : H + 1], d_embed,
        d_second, d_bias, d_first[: EIN + 1],
    )


def on_device(
    node_feat, dist_feat, bond, source, target_node, mol_id, flag, target,
    embed_weight, edge_first, edge_second, gru_weight, set_lstm, head_weight,
    mom_embed, mom_first, mom_second, mom_gru, mom_lstm, mom_head,
    var_embed, var_first, var_second, var_gru, var_lstm, var_head, step_count,
    *, sizes,
):
    width = embed_weight.shape[1]
    gates = H // width
    mine = lax.axis_index("gate")
    columns = jnp.arange(NT)[None, :]
    present = jnp.maximum(flag[:, None], (columns < NT // 2).astype(jnp.int32)).astype(F32)
    count = lax.psum(jnp.sum(present), ("grp", "edge"))
    inverse = (1.0 / count).reshape(1)

    low_second = edge_second[:EDGE_HID].astype(BF).T
    gru_low = gru_weight[:, :H].astype(BF).transpose(0, 2, 3, 1)
    parts = [
        low_second,
        exact3(edge_second[EDGE_HID]),
        gru_low,
        exact3(gru_weight[:, H]),
        embed_weight.astype(BF).T,
    ]
    lengths = [up(part.size, H) // H for part in parts]
    rows = up(sum(lengths), 32)
    packed = lax.all_gather(pack_rows(parts, rows), "gate", axis=0, tiled=False)
    begins = [sum(lengths[:index]) for index in range(len(lengths) + 1)]
    pieces = [
        packed[:, begins[index] : begins[index + 1]].reshape(gates, -1)[:, : part.size].reshape((gates,) + part.shape)
        for index, part in enumerate(parts)
    ]
    second = pieces[0]
    bias = jnp.sum(pieces[1].astype(F32), axis=1).reshape(gates, width, H).transpose(0, 2, 1)
    gru = pieces[2].transpose(1, 2, 0, 3, 4).reshape(2, 3 * H, H)
    gru_bias = jnp.sum(pieces[3].astype(F32), axis=1).transpose(1, 2, 0, 3).reshape(2, 3 * H, 1)
    embed_t = pieces[4].reshape(H, -1)

    loss, d_lstm, d_head, d_gru, d_embed, d_second, d_bias, d_first = local_part(
        mine.reshape(1), node_feat, dist_feat, bond, source, target_node, mol_id, present, target, inverse,
        gates, embed_t, second, bias, gru, gru_bias, edge_first, set_lstm, head_weight,
    )
    everywhere = ("grp", "edge", "gate")
    own = lax.psum_scatter(d_second, "gate", scatter_dimension=0, tiled=False)
    own = lax.psum(own, ("grp", "edge"))
    loss, d_lstm, d_head, d_gru, d_embed, d_bias, d_first = lax.psum(
        (loss, d_lstm, d_head, d_gru, d_embed, d_bias, d_first), everywhere
    )
    d_bias = lax.dynamic_slice_in_dim(d_bias, mine * width, width, 0).reshape(1, width * H)
    grad_second = jnp.concatenate([own.T, d_bias], axis=0)
    grad_gru = lax.dynamic_slice_in_dim(d_gru.reshape(2, H + 1, 3, H), mine * width, width, 3)
    grad_embed = lax.dynamic_slice_in_dim(d_embed, mine * width, width, 1)
    grads = (grad_embed, d_first, grad_second, grad_gru, d_lstm, d_head)
    split_sq = jnp.sum(own * own)
    whole_sq = (
        jnp.sum(d_embed * d_embed) + jnp.sum(d_gru * d_gru) + jnp.sum(d_lstm * d_lstm)
        + jnp.sum(d_head * d_head) + jnp.sum(d_first * d_first)
    )
    bias_sq = jnp.sum(d_bias * d_bias)
    norm = jnp.sqrt(lax.psum(split_sq + bias_sq, "gate") + whole_sq)
    factor = jnp.minimum(1.0, CLIP / norm)
    params = (embed_weight, edge_first, edge_second, gru_weight, set_lstm, head_weight)
    moms = (mom_embed, mom_first, mom_second, mom_gru, mom_lstm, mom_head)
    varis = (var_embed, var_first, var_second, var_gru, var_lstm, var_head)
    stepno = step_count[0].astype(F32)
    results = [
        adamw(params[index], grads[index] * factor, moms[index], varis[index], RATES[index], stepno)
        for index in range(6)
    ]
    return (loss, norm) + tuple(results[index][kind] for kind in range(3) for index in range(6))


def solution(mesh):
    rows = P(("grp", "edge"), None)
    line = P(("grp", "edge"))
    cols = P(None, "gate")
    deep = P(None, None, None, "gate")
    weights = (cols, P(), cols, deep, P(), P())
    return jax.shard_map(
        functools.partial(on_device, sizes=dict(mesh.shape)),
        mesh=mesh,
        in_specs=(rows, rows, line, line, line, line, line, rows) + weights * 3 + (P(),),
        out_specs=(P(), P()) + weights * 3,
        check_vma=False,
    )
```

time: 1630 us -> 720 us (0.44); the launches traced: 1600 us -> 720 us
  matrix products: 553 us -> 0 us
  other arithmetic: 421 us -> 27.1 us
  local copies, waits for them, and re-layouts: 339 us -> 38.3 us
  Pallas kernels: 0 us -> 246 us
  waiting for transfers between devices: 112 us -> 313 us
  blocking collectives: 145 us -> 72.5 us
    dot_general x263 -> x0, matrix products: 553 us -> none  [the longest x39 140 us: send_one_block(): jnp.einsum('eoi,ei->eo', mats, hidden_full[src_rows], preferred_element_t...]
    pallas_call x0 -> x5, Pallas kernels: none -> 246 us  [the longest x1 90.6 us: backward(): pl.pallas_call(functools.partial(backward_kernel, chunks=second.shape[0])...]
    scatter-add x78 -> x0, other arithmetic: 245 us -> none  [the longest x39 125 us: return_one_block(): jax.ops.segment_sum(parts, src_rows, num_segments=nodes)]
    gather x104 -> x0, local copies, waits for them, and re-layouts: 208 us -> none  [the longest x39 56.4 us: return_one_block(): d_msg_low[tgt_rows]]
    psum x1 -> x2, waiting for transfers between devices: 0.01 us -> 148 us  [the longest x1 90.5 us: on_device(): lax.psum((loss, d_lstm, d_head, d_gru, d_embed, d_bias, d_first), everywh...]
    unnamed x7 -> x5, waiting for transfers between devices: 0.12 us -> 144 us
    reduce_scatter x6 -> x0, waiting for transfers between devices: 112 us -> none  [the longest x3 70.5 us: on_device(): lax.psum_scatter(ndot(d_gin_low, gru_low[0]), 'gate', scatter_dimension=1...]
    all_gather x7 -> x0, blocking collectives: 73.8 us -> none  [the longest x4 41.1 us: gather_hidden(): lax.all_gather(state.astype(jnp.bfloat16), 'gate', axis=1, tiled=True)]
  transfers between devices with their start and end apart: 7 -> 4, of which waited for: 6 -> 4; matrix products, arithmetic and copies ran while one was open for 10% -> 3% of each run, Pallas kernels for 0% -> 1%
where the time goes in v1:
time: 720 us
  waiting for transfers between devices  313 us (43%)
  Pallas kernels  246 us (34%)
  blocking collectives  72.5 us (10%)
  local copies, waits for them, and re-layouts  38.3 us (5%)
  other arithmetic  27.1 us (4%)
  between operations  22.2 us (3%)
    unnamed x5, waiting for transfers between devices  144 us
    pallas_call x1, Pallas kernels, backward(): pl.pallas_call(functools.partial(backward_kernel, chunks=second.shape[0])...  90.6 us
    psum x1, waiting for transfers between devices, on_device(): lax.psum((loss, d_lstm, d_head, d_gru, d_embed, d_bias, d_first), everywh...  90.5 us
    pallas_call x1, Pallas kernels, forward(): pl.pallas_call(functools.partial(forward_kernel, chunks=chunks), out_shap...  85.7 us
    psum x1, waiting for transfers between devices, on_device(): own = lax.psum(own, ('grp', 'edge'))  57.4 us
    psum x1, blocking collectives, on_device(): lax.psum((loss, d_lstm, d_head, d_gru, d_embed, d_bias, d_first), everywh...  43.1 us
    pallas_call x1, Pallas kernels, edge_grads(): pl.pallas_call(functools.partial(final_kernel, chunks=chunks, group=8), o...  32.1 us
    pallas_call x1, Pallas kernels, readout(): pl.pallas_call(readout_kernel, out_shape=(jax.ShapeDtypeStruct((8, H), F3...  30.7 us
  transfers between devices with their start and end apart: 4, of which 4 were waited for; matrix products, arithmetic and copies ran while one was open for 3% of the time, Pallas kernels for 1%

profile of v1, /device:TPU:0, one launch (start us, length us, event | category | flops | bytes accessed | tf_op | source)
XLA Modules:
  0.0 719.5 jit_solution(1972593381391241138)
XLA Ops:
  7.3 1.7 fusion.1
  9.0 0.9 reduce-precision_convert_fusion.3
  9.9 0.9 slice.88
  11.9 1.0 concatenate.11
  12.9 1.1 copy.201
  14.0 1.1 pad.54.clone
  16.0 19.1 %psum.70 = f32[]{:T(128)} all-reduce(f32[]{:T(128)} %fusion.6), channel_id=1, replica_groups=mesh['grp'=2,'edge'=4,'gate'=4] {'grp','edge'}, use_global_device_ids=true, to_apply=%region_1.0 | all-reduce | flops 1 | bytes 8 | tf_op jit(solution)/shard_map/psum | solution.py:677
  36.6 1.9 concatenate.10
  39.1 1.3 pad.50.data
  40.5 0.8 copy.174
  42.0 0.9 pad.55.lstm
  45.8 7.2 %prep.1 = (s32[8]{0:T(128)}, f32[128,5120]{1,0:T(8,128)}, bf16[128,5120]{1,0:T(8,128)(2,1)}, bf16[5120,128]{1,0:T(8,128)(2,1)}, bf16[32,5120]{1,0:T(8,128)(2,1)}, /*index=5*/s32[8,5120]{1,0:T(8,128)}) custom-call(s32[1]{0:T(128)} %bitcast.place, s32[1,2560]{1,0:T(1,128)} %reshape.154.mol, s32[32,256]{1,0:T(8,128)} %pad.49.src2d, ...), custom_call_target="tpu_custom_call" | custom-call | tf_op jit(solution)/shard_map/prep/pallas_call | solution.py:149
  53.0 20.6 %all-gather.3.cloned.1.call-done = bf16[17664,128]{1,0:T(8,128)(2,1)} async-done(((bf16[4416,128]{1,0:T(8,128)(2,1)}), bf16[17664,128]{1,0:T(8,128)(2,1)}) %all-gather.3.cloned.1.call-update) | async-done | bytes 4522000 | tf_op jit(solution)/shard_map/all_gather | solution.py:691
  73.5 0.7 slice.68
  74.3 4.4 slice.69.second
  78.7 0.9 slice_convert_fusion.1
  79.6 0.9 slice.71
  80.6 0.7 slice_bitcast_fusion.1
  81.3 0.7 reshape_reshape_reshape.3.embed
  82.2 0.8 copy.183
  83.9 1.1 reshape.170.gru_bias
  85.1 85.7 %forward.1 = (bf16[4,128,2560]{2,1,0:T(8,128)(2,1)}, bf16[3,128,2560]{2,1,0:T(8,128)(2,1)}, f32[3,128,2560]{2,1,0:T(8,128)}, bf16[3,128,5120]{2,1,0:T(8,128)(2,1)}) custom-call(s32[8]{0:T(128)} %get-tuple-element.40.scal, bf16[16,2560]{1,0:T(8,128)(2,1)} %pad.52.nf_t, bf16[128,16]{1,0:T(8,128)(2,1)} %reshape_reshape_reshape.3.embed, ...), custom_call_target="tpu_custom_call" | custom-call | tf_op jit(solution)/shard_map/forward/pallas_call | solution.py:256
  170.8 2.0 slice_bitcast_fusion.final
  172.8 30.7 %readout.1 = (f32[8,128]{1,0:T(8,128)}, f32[128,2560]{1,0:T(8,128)}, f32[392,512]{1,0:T(8,128)}, f32[264,128]{1,0:T(8,128)}) custom-call(s32[8]{0:T(128)} %get-tuple-element.40.scal, f32[1]{0:T(128)} %bitcast.6.inverse, bf16[128,2560]{1,0:T(8,128)(2,1)} %slice_bitcast_fusion.final, s32[1,2560]{1,0:T(1,128)} %reshape.154.mol, f32[392,512]{1,0:T(8,128)} %pad.55.lstm, ...), custom_call_target="tpu_custom_call" | custom-call | tf_op jit(solution)/shard_map/readout/pallas_call | solution.py:393
  203.5 90.6 %backward.1 = (bf16[3,128,5120]{2,1,0:T(8,128)(2,1)}, f32[2,144,384]{2,1,0:T(8,128)}, f32[16,128]{1,0:T(8,128)}) custom-call(s32[8]{0:T(128)} %get-tuple-element.40.scal, bf16[16,2560]{1,0:T(8,128)(2,1)} %pad.52.nf_t, bf16[4,4096,128]{2,1,0:T(8,128)(2,1)} %slice.69.second, f32[4,128,32]{2,1,0:T(8,128)} %bitcast.63, bf16[2,384,128]{2,1,0:T(8,128)(2,1)} %bitcast.65, ...), custom_call_target="tpu_custom_call" | custom-call | tf_op jit(solution)/shard_map/backward/pallas_call | solution.py:491
  294.1 32.1 %edge_grads.1 = (f32[4,4096,128]{2,1,0:T(8,128)}, f32[128,128]{1,0:T(8,128)}, f32[32,128]{1,0:T(8,128)}) custom-call(s32[8]{0:T(128)} %get-tuple-element.40.scal, bf16[4,4096,128]{2,1,0:T(8,128)(2,1)} %slice.69.second, bf16[3,128,5120]{2,1,0:T(8,128)(2,1)} %get-tuple-element.45.near, bf16[3,128,5120]{2,1,0:T(8,128)(2,1)} %get-tuple-element.49.far, ...), custom_call_target="tpu_custom_call" | custom-call | tf_op jit(solution)/shard_map/edge_grads/pallas_call | solution.py:567
  326.3 0.9 copy-done.6
  327.3 0.8 slice.62
  328.1 144.2 %reduce-scatter.4.cloned.1.call-done = f32[1,4096,128]{2,1,0:T(8,128)} async-done(((f32[4,4096,128]{2,1,0:T(8,128)}), f32[1,4096,128]{2,1,0:T(8,128)}) %reduce-scatter.4.cloned.1.call-update) | async-done | bytes 2097168
  472.4 2.9 copy.190
  476.3 1.2 slice.61
  477.5 43.1 %all-reduce.13 = (f32[]{:T(128)}, f32[16,128]{1,0:T(8,128)S(1)}, f32[257,12]{1,0:T(8,128)S(1)}, f32[17,128]{1,0:T(8,128)S(1)}) all-reduce(f32[]{:T(128)} %bitcast.21, f32[16,128]{1,0:T(8,128)S(1)} %copy-done.24, f32[257,12]{1,0:T(8,128)S(1)} %bitcast.73, ...), channel_id=1, replica_groups=mesh['grp'=2,'edge'=4,'gate'=4] {'grp','edge','gate'}, use_global_device_ids=true, to_apply=%region_4.5 | all-reduce | flops 7309 | bytes 58472 | tf_op jit(solution)/shard_map/psum | solution.py:710
  522.4 90.5 %all-reduce.20.cloned.1.call-done = (f32[128,128]{1,0:T(8,128)}, f32[2,129,384]{2,1,0:T(8,128)}, f32[385,512]{1,0:T(8,128)}) async-done(((f32[128,128]{1,0:T(8,128)}, f32[2,129,384]{2,1,0:T(8,128)}, f32[385,512]{1,0:T(8,128)}), (f32[128,128]{1,0:T(8,128)}, f32[2,129,384]{2,1,0:T(8,128)}, f32[385,512]{1,0:T(8,128)})) %all-reduce.20.cloned.1.call-update) | async-done | bytes 1250320 | tf_op jit(solution)/shard_map/psum | solution.py:710
  613.0 1.3 copy.200
  614.3 1.7 multiply_reduce_fusion.2
  617.3 2.0 multiply_reduce_fusion.1
  620.6 1.9 multiply_reduce_fusion.4
  622.6 57.4 %all-reduce.18.cloned.1.call-done = f32[4096,128]{0,1:T(8,128)} async-done(((f32[4096,128]{0,1:T(8,128)}), f32[4096,128]{0,1:T(8,128)}) %all-reduce.18.cloned.1.call-update) | async-done | bytes 2097168 | tf_op jit(solution)/shard_map/psum | solution.py:709
  680.0 2.7 multiply_reduce_fusion
  684.7 10.3 %psum.74 = f32[]{:T(128)} all-reduce(f32[]{:T(128)S(6)} %add.168), channel_id=1, replica_groups=mesh['grp'=2,'edge'=4,'gate'=4] {'gate'}, use_global_device_ids=true, to_apply=%region_10.11 | all-reduce | flops 1 | bytes 8 | tf_op jit(solution)/shard_map/psum | solution.py:724
  695.9 0.7 copy.197
  696.6 0.7 copy.198
  697.3 0.7 copy.199
  698.1 1.4 multiply_subtract_fusion.5
  699.5 1.4 multiply_subtract_fusion.4
  700.9 3.4 multiply_subtract_fusion.1
  704.3 1.9 multiply_subtract_fusion.2
  706.2 5.6 multiply_subtract_fusion
  (117 shorter events, 10.2 us)
Async XLA Ops:
  7.2 4.0 slice-start
  7.2 4.4 copy-start.13
  7.2 66.3 %all-gather.3.cloned.1.call-start = ((), (), s32[]{:S(2)}) async-start(), calls=%async_computation.2 | async-start | bytes 5652480 | tf_op jit(solution)/shard_map/all_gather | solution.py:691
  14.0 1.3 copy-start.25
  14.0 21.1 %copy-start.21 = (s32[2432]{0:T(1024)S(1)}, s32[2432]{0:T(1024)}, u32[]{:S(2)}) copy-start(s32[2432]{0:T(1024)} %param.32) | copy-start | bytes 29188
  14.0 21.7 %copy-start.9 = (s32[4992]{0:T(1024)S(1)}, s32[4992]{0:T(1024)}, u32[]{:S(2)}) copy-start(s32[4992]{0:T(1024)} %param.30) | copy-start | bytes 59908
  14.0 22.4 %copy-start.19 = (s32[4992]{0:T(1024)S(1)}, s32[4992]{0:T(1024)}, u32[]{:S(2)}) copy-start(s32[4992]{0:T(1024)} %param.31) | copy-start | bytes 59908
  14.0 22.5 %copy-start.20 = (s32[4992]{0:T(1024)S(1)}, s32[4992]{0:T(1024)}, u32[]{:S(2)}) copy-start(s32[4992]{0:T(1024)} %param.29) | copy-start | bytes 59908
  14.0 22.5 %copy-start.7 = (bf16[4992,12]{0,1:T(8,128)(2,1)S(1)}, bf16[4992,12]{0,1:T(8,128)(2,1)}, u32[]{:S(2)}) copy-start(bf16[4992,12]{0,1:T(8,128)(2,1)} %param.28) | copy-start | bytes 359428
  15.2 457.1 %reduce-scatter.4.cloned.1.call-start = ((), (), s32[]{:S(2)}) async-start(), calls=%async_computation.3 | async-start | bytes 10485760
  36.6 3.9 copy-start.12
  38.4 2.8 copy-start.10
  38.4 3.4 copy-start.16
  38.5 3.5 copy-start.2
  39.1 5.2 copy-start.23
  326.3 1.0 copy-start.6
  326.3 286.7 %all-reduce.20.cloned.1.call-start = ((), (), s32[]{:S(2)}) async-start(), calls=%async_computation.4 | async-start | bytes 2572288 | tf_op jit(solution)/shard_map/psum | solution.py:710
  328.1 148.0 %copy-start.17 = (f32[257,12]{0,1:T(8,128)S(1)}, f32[257,12]{0,1:T(8,128)}, u32[]{:S(2)}) copy-start(f32[257,12]{0,1:T(8,128)} %param.52) | copy-start | bytes 37012
  328.1 148.1 %copy-start.18 = (f32[257,12]{0,1:T(8,128)S(1)}, f32[257,12]{0,1:T(8,128)}, u32[]{:S(2)}) copy-start(f32[257,12]{0,1:T(8,128)} %param.46) | copy-start | bytes 37012
  328.1 351.9 %all-reduce.18.cloned.1.call-start = ((), (), s32[]{:S(2)}) async-start(), calls=%async_computation.1 | async-start | bytes 4194304 | tf_op jit(solution)/shard_map/psum | solution.py:709
  475.2 2.3 copy-start.22
  475.2 2.3 copy-start.8
  475.2 2.3 copy-start.24
  520.6 93.7 %copy-start.15 = (f32[16,128]{1,0:T(8,128)}, f32[16,128]{1,0:T(8,128)S(1)}, u32[]{:S(2)}) copy-start(f32[16,128]{1,0:T(8,128)S(1)} %get-tuple-element.161) | copy-start | bytes 24580
  616.0 82.1 %copy-start.14 = (f32[16,32]{1,0:T(8,128)S(1)}, f32[16,32]{1,0:T(8,128)}, u32[]{:S(2)}) copy-start(f32[16,32]{1,0:T(8,128)} %param.35) | copy-start | bytes 6148
  617.3 83.6 %copy-start.3 = (f32[385,512]{1,0:T(8,128)S(1)}, f32[385,512]{1,0:T(8,128)}, u32[]{:S(2)}) copy-start(f32[385,512]{1,0:T(8,128)} %get-tuple-element.166) | copy-start | bytes 2365444
  695.8 8.5 %copy-start.5 = (f32[2,129,3,32]{1,3,2,0:T(8,128)S(1)}, f32[2,129,3,32]{1,3,2,0:T(8,128)}, u32[]{:S(2)}) copy-start(f32[2,129,3,32]{1,3,2,0:T(8,128)} %param.38) | copy-start | bytes 297220
  700.9 5.3 copy-start
  700.9 5.3 copy-start.1
  700.9 5.3 copy-start.4
  700.9 5.3 copy-start.11
Sparse Core Ops, SparseCore 0:
  15.3 58.1 all-gather.2
  326.4 145.9 reduce-scatter.3
  480.4 132.5 all-reduce.19
  615.9 64.0 all-reduce.17
